TPU v7x, 32 devices: a whole 2x2x4 slice. The times are simulated.
32 devices in a mesh: row: 8 (over y, x, core), section: 4 (over z).
Axes of the slice: x: 2, y: 2, z: 4, core: 2. Of those that a mesh axis runs over, the one named last changes fastest.
Arguments:
- features: bfloat16 [8192, 256], P('row'), may hold values from -6 to 6
- weight: bfloat16 [256, 256], replicated, may hold values from -0.375 to 0.375
- cotangent: bfloat16 [8192, 256], P('row'), may hold values from -0.0625 to 0.0625
- counts: int32 [64, 16, 128, 128], P('row', 'section'), may hold values from 0 to 3, as said below
- columns: int32 [64, 16], P('row', 'section'), may hold values from 0 to 63, as said below
- live_slots: int32 [64, 4], P('row', 'section'), may hold values from 1 to 4, as said below
Outputs:
- output: bfloat16 [8192, 256], P('row')
- grad_weight: float32 [256, 256], replicated
Inputs may be any that keep to these rules, and one draw needn't show every extreme that they name: `columns`: every entry in a slot of section index s names a node block g with (g // 8) % 4 == s; the 4 slots of one row of blocks and one section index name distinct column blocks. Slots at k >= live_slots[b, s] are ignored; the value 4 occurs at every section index in every draw. `counts`: most entries are zero.
All inputs are finite; a program needn't handle non-finite values.
Results may differ from a plain program's by a relative error of at most 0.0055.
Values may be sent and summed in bfloat16 or wider, within the bound.
A program may use at most 64 MiB of HBM per device.

v0:
```python
import jax
import jax.numpy as jnp
from jax import lax
from jax.sharding import PartitionSpec as P


def per_device(features, weight, cotangent, counts, columns, live_slots):
    row_count = features.shape[0]
    feat_width = features.shape[1]
    block_count = columns.shape[0]
    slot_count = columns.shape[1]
    block_size = counts.shape[2]
    section_index = lax.axis_index("section")
    section_count = lax.axis_size("section")
    owner_count = lax.axis_size("row") // section_count
    everything = lax.all_gather(features, "row", axis=0, tiled=True)
    grouped = everything.reshape(owner_count, section_count, row_count, feat_width)
    window = lax.dynamic_index_in_dim(grouped, section_index, 1, keepdims=False)
    window = window.reshape(owner_count * block_count, block_size, feat_width)
    local_cols = columns // block_count // section_count * block_count + columns % block_count
    slot_used = jnp.arange(slot_count, dtype=jnp.int32)[None, :] < live_slots
    masked = jnp.where(slot_used[:, :, None, None], counts, 0)
    degree = jnp.sum(masked, axis=(1, 3)).astype(jnp.float32).reshape(row_count)
    edge_mats = masked.astype(jnp.bfloat16)
    picked = window[local_cols]
    partial_value = jnp.einsum(
        "rkij,rkjf->rif", edge_mats, picked, preferred_element_type=jnp.float32
    )
    partial_value = partial_value.reshape(row_count, feat_width)
    summed, degree_all = lax.psum((partial_value, degree), "section")
    aggregate = (summed * lax.rsqrt(1.0 + degree_all)[:, None]).astype(jnp.bfloat16)
    pre_act = jnp.dot(aggregate, weight, preferred_element_type=jnp.float32)
    gate_value = jax.nn.sigmoid(pre_act)
    output = (pre_act * gate_value).astype(jnp.bfloat16)
    grad_pre = (
        cotangent.astype(jnp.float32) * gate_value * (1.0 + pre_act * (1.0 - gate_value))
    ).astype(jnp.bfloat16)
    grad_local = lax.dot_general(
        aggregate, grad_pre, (((0,), (0,)), ((), ())), preferred_element_type=jnp.float32
    )
    grad_weight = lax.psum(grad_local, "row")
    return (output, grad_weight)


def solution(mesh):
    in_specs = (
        P("row", None),
        P(),
        P("row", None),
        P("row", "section", None, None),
        P("row", "section"),
        P("row", "section"),
    )
    out_specs = (P("row", None), P())
    return jax.shard_map(
        per_device, mesh=mesh, in_specs=in_specs, out_specs=out_specs, check_vma=False
    )
```

profile of v0, /device:TPU:0, one launch (start us, length us, event | category | flops | bytes accessed | tf_op | source)
XLA Modules:
  0.0 172.0 jit_solution(4953633193396426414)
XLA Ops:
  7.2 0.0 copy-start
  7.2 0.0 all-gather.2.cloned.1.call-start
  7.2 0.7 all-gather.2.cloned.1.call-update
  7.9 0.0 all-reduce.3.cloned.1.call-start
  8.0 0.7 compare_select_fusion
  8.7 0.1 copy.9
  8.8 0.1 reshape.45
  8.8 0.7 iota_compare_fusion
  9.6 39.8 %all-gather.2.cloned.1.call-done = bf16[8192,256]{1,0:T(8,128)(2,1)} async-done(((bf16[1024,256]{1,0:T(8,128)(2,1)}), bf16[8192,256]{1,0:T(8,128)(2,1)}) %all-gather.2.cloned.1.call-update) | async-done | bytes 4194320 | tf_op jit(solution)/shard_map/all_gather | solution.py:16
  49.4 1.3 constant_dynamic-slice_fusion
  50.6 0.7 gather_fusion
  51.3 3.2 %fusion = f32[8,128,256,1]{2,1,3,0:T(8,128)} fusion(bf16[8,4,128,256]{3,2,1,0:T(8,128)(2,1)S(1)} %bitcast.13, s32[8,4,128,128]{3,2,1,0:T(8,128)} %param.9, pred[8,4]{1,0:T(8,128)(4,1)S(1)} %iota_compare_fusion), kind=kOutput, calls=%fused_computation.3 | convolution fusion | flops 269484032 | bytes 5242912 | tf_op jit(solution)/shard_map/rkij,rkjf->rif/dot_general | solution.py:26
  54.5 0.0 all-reduce.3.cloned.1.call-update
  54.5 0.0 all-reduce.5.cloned.1.call-start
  54.6 1.9 %select_reduce_fusion = s32[8,128]{1,0:T(8,128)S(1)} fusion(s32[8,4,128,128]{3,2,1,0:T(8,128)} %param.9, pred[8,4]{1,0:T(8,128)(4,1)S(1)} %iota_compare_fusion), kind=kLoop, calls=%fused_computation.1 | loop fusion | flops 1047552 | bytes 2101280 | tf_op jit(solution)/shard_map/reduce_sum | solution.py:23
  56.5 11.9 %psum.22 = f32[1024]{0:T(1024)S(1)} all-reduce(f32[1024]{0:T(1024)S(1)} %convert_bitcast_fusion), channel_id=1, replica_groups=mesh['row'=8,'section'=4] {'section'}, use_global_device_ids=true, to_apply=%region_2.3 | all-reduce | flops 1024 | bytes 8192 | tf_op jit(solution)/shard_map/psum | solution.py:30
  68.5 0.0 copy-start.2
  68.5 38.2 %all-reduce.3.cloned.1.call-done = f32[1024,256]{1,0:T(8,128)} async-done(((f32[1024,256]{1,0:T(8,128)}), f32[1024,256]{1,0:T(8,128)}) %all-reduce.3.cloned.1.call-update) | async-done | bytes 1048592 | tf_op jit(solution)/shard_map/psum | solution.py:30
  106.6 0.0 copy-done
  106.6 0.0 copy-start.1
  106.6 2.6 %multiply_convert_fusion.1 = (bf16[1024,256]{1,0:T(8,128)(2,1)}, f32[1024,256]{1,0:T(8,128)S(1)}) fusion(bf16[256,256]{1,0:T(8,128)(2,1)S(1)} %copy-done, f32[1024,256]{1,0:T(8,128)} %all-reduce.3.cloned.1.call-done, f32[1024]{0:T(1024)S(1)} %add_rsqrt_fusion), kind=kOutput, calls=%fused_computation.5 | convolution fusion | flops 136052736 | bytes 2756608 | tf_op jit(solution)/shard_map/dot_general | solution.py:32
  109.2 0.0 copy-done.2
  109.2 0.0 copy-done.1
  109.2 1.5 fusion.3
  110.7 0.0 all-reduce.5.cloned.1.call-update
  110.7 53.1 %all-reduce.5.cloned.1.call-done = f32[256,256]{1,0:T(8,128)} async-done(((f32[256,256]{1,0:T(8,128)}), f32[256,256]{1,0:T(8,128)}) %all-reduce.5.cloned.1.call-update) | async-done | bytes 262160 | tf_op jit(solution)/shard_map/psum | solution.py:41
  163.8 1.7 copy.13
  (3 shorter events, 0.0 us)
Async XLA Ops:
  7.2 99.5 %copy-start = (bf16[256,256]{1,0:T(8,128)(2,1)S(1)}, bf16[256,256]{1,0:T(8,128)(2,1)}, u32[]{:S(2)}) copy-start(bf16[256,256]{1,0:T(8,128)(2,1)} %param.7) | copy-start | bytes 393220
  7.2 42.2 %all-gather.2.cloned.1.call-start = ((), (), s32[]{:S(2)}) async-start(), calls=%async_computation | async-start | bytes 4718592 | tf_op jit(solution)/shard_map/all_gather | solution.py:16
  7.9 98.7 %all-reduce.3.cloned.1.call-start = ((), (), s32[]{:S(2)}) async-start(), calls=%async_computation.1 | async-start | bytes 2097152 | tf_op jit(solution)/shard_map/psum | solution.py:30
  54.5 109.3 %all-reduce.5.cloned.1.call-start = ((), (), s32[]{:S(2)}) async-start(), calls=%async_computation.2 | async-start | bytes 524288 | tf_op jit(solution)/shard_map/psum | solution.py:41
  68.5 40.8 %copy-start.2 = (bf16[1024,256]{1,0:T(8,128)(2,1)S(1)}, bf16[1024,256]{1,0:T(8,128)(2,1)}, u32[]{:S(2)}) copy-start(bf16[1024,256]{1,0:T(8,128)(2,1)} %param.8) | copy-start | bytes 1572868
  106.6 2.6 %copy-start.1 = (f32[1024,256]{1,0:T(8,128)S(1)}, f32[1024,256]{1,0:T(8,128)}, u32[]{:S(2)}) copy-start(f32[1024,256]{1,0:T(8,128)} %all-reduce.3.cloned.1.call-done) | copy-start | bytes 3145732
Sparse Core Ops, SparseCore 0:
  9.9 39.4 all-gather.1
  54.7 51.9 all-reduce.2
  110.8 52.9 all-reduce.4
where the time goes:
time: 172 us
  waiting for transfers between devices  132 us (77%)
  between operations  13.8 us (8%)
  blocking collectives  11.9 us (7%)
  matrix products  7.25 us (4%)
  local copies, waits for them, and re-layouts  3.82 us (2%)
  other arithmetic  3.35 us (2%)
    psum x1, waiting for transfers between devices, per_device(): grad_weight = lax.psum(grad_local, 'row')  53.1 us
    all_gather x1, waiting for transfers between devices, per_device(): everything = lax.all_gather(features, 'row', axis=0, tiled=True)  39.8 us
    psum x1, waiting for transfers between devices, per_device(): summed, degree_all = lax.psum((partial_value, degree), 'section')  38.2 us
    psum x1, blocking collectives, per_device(): summed, degree_all = lax.psum((partial_value, degree), 'section')  11.9 us
  transfers between devices with their start and end apart: 3, of which 3 were waited for; matrix products, arithmetic and copies ran while one was open for 2% of the time, Pallas kernels for 0%

commit v1 on v0

--- a/solution.py
+++ b/solution.py
@@ -38,7 +38,8 @@
     grad_local = lax.dot_general(
         aggregate, grad_pre, (((0,), (0,)), ((), ())), preferred_element_type=jnp.float32
     )
-    grad_weight = lax.psum(grad_local, "row")
+    shards = lax.all_gather(grad_local, "row", axis=0, tiled=False)
+    grad_weight = shards.sum(axis=0)
     return (output, grad_weight)
 
 

time: 172 us -> 147 us (0.85)
  waiting for transfers between devices: 132 us -> 106 us
  other arithmetic: 3.35 us -> 5.8 us
    psum x1 -> x0, waiting for transfers between devices: 53.1 us -> none  [per_device(): grad_weight = lax.psum(grad_local, 'row')]
    all_gather x0 -> x1, waiting for transfers between devices: none -> 27.4 us  [per_device(): shards = lax.all_gather(grad_local, 'row', axis=0, tiled=False)]
    reduce_sum x0 -> x1, other arithmetic: none -> 2.45 us  [per_device(): grad_weight = shards.sum(axis=0)]
where the time goes in v1:
time: 147 us
  waiting for transfers between devices  106 us (72%)
  between operations  13.8 us (9%)
  blocking collectives  11.9 us (8%)
  matrix products  7.25 us (5%)
  other arithmetic  5.8 us (4%)
  local copies, waits for them, and re-layouts  2.16 us (1%)
    all_gather x1, waiting for transfers between devices, per_device(): everything = lax.all_gather(features, 'row', axis=0, tiled=True)  39.8 us
    psum x1, waiting for transfers between devices, per_device(): summed, degree_all = lax.psum((partial_value, degree), 'section')  38.2 us
    all_gather x1, waiting for transfers between devices, per_device(): shards = lax.all_gather(grad_local, 'row', axis=0, tiled=False)  27.4 us
    psum x1, blocking collectives, per_device(): summed, degree_all = lax.psum((partial_value, degree), 'section')  11.9 us
    dot_general x1, matrix products, per_device(): jnp.einsum('rkij,rkjf->rif', edge_mats, picked, preferred_element_type=jn...  3.18 us
  transfers between devices with their start and end apart: 3, of which 3 were waited for; matrix products, arithmetic and copies ran while one was open for 2% of the time, Pallas kernels for 0%

profile of v1, /device:TPU:0, one launch (start us, length us, event | category | flops | bytes accessed | tf_op | source)
XLA Modules:
  0.0 147.1 jit_solution(10636196471126940694)
XLA Ops:
  7.2 0.0 copy-start
  7.2 0.0 all-gather.4.cloned.1.call-start
  7.2 0.7 all-gather.4.cloned.1.call-update
  7.9 0.0 all-reduce.2.cloned.1.call-start
  8.0 0.7 compare_select_fusion
  8.7 0.1 copy.9
  8.8 0.1 reshape.45
  8.8 0.7 iota_compare_fusion
  9.6 39.8 %all-gather.4.cloned.1.call-done = bf16[8192,256]{1,0:T(8,128)(2,1)} async-done(((bf16[1024,256]{1,0:T(8,128)(2,1)}), bf16[8192,256]{1,0:T(8,128)(2,1)}) %all-gather.4.cloned.1.call-update) | async-done | bytes 4194320 | tf_op jit(solution)/shard_map/all_gather | solution.py:16
  49.4 1.3 constant_dynamic-slice_fusion
  50.6 0.7 gather_fusion
  51.3 3.2 %fusion = f32[8,128,256,1]{2,1,3,0:T(8,128)} fusion(bf16[8,4,128,256]{3,2,1,0:T(8,128)(2,1)S(1)} %bitcast.14, s32[8,4,128,128]{3,2,1,0:T(8,128)} %param.9, pred[8,4]{1,0:T(8,128)(4,1)S(1)} %iota_compare_fusion), kind=kOutput, calls=%fused_computation.3 | convolution fusion | flops 269484032 | bytes 5242912 | tf_op jit(solution)/shard_map/rkij,rkjf->rif/dot_general | solution.py:26
  54.5 0.0 all-reduce.2.cloned.1.call-update
  54.5 0.0 all-gather.6.cloned.1.call-start
  54.6 1.9 %select_reduce_fusion = s32[8,128]{1,0:T(8,128)S(1)} fusion(s32[8,4,128,128]{3,2,1,0:T(8,128)} %param.9, pred[8,4]{1,0:T(8,128)(4,1)S(1)} %iota_compare_fusion), kind=kLoop, calls=%fused_computation.1 | loop fusion | flops 1047552 | bytes 2101280 | tf_op jit(solution)/shard_map/reduce_sum | solution.py:23
  56.5 11.9 %psum.15 = f32[1024]{0:T(1024)S(1)} all-reduce(f32[1024]{0:T(1024)S(1)} %convert_bitcast_fusion), channel_id=1, replica_groups=mesh['row'=8,'section'=4] {'section'}, use_global_device_ids=true, to_apply=%region_2.3 | all-reduce | flops 1024 | bytes 8192 | tf_op jit(solution)/shard_map/psum | solution.py:30
  68.5 0.0 copy-start.2
  68.5 38.2 %all-reduce.2.cloned.1.call-done = f32[1024,256]{1,0:T(8,128)} async-done(((f32[1024,256]{1,0:T(8,128)}), f32[1024,256]{1,0:T(8,128)}) %all-reduce.2.cloned.1.call-update) | async-done | bytes 1048592 | tf_op jit(solution)/shard_map/psum | solution.py:30
  106.6 0.0 copy-done
  106.6 0.0 copy-start.1
  106.6 2.6 %multiply_convert_fusion.1 = (bf16[1024,256]{1,0:T(8,128)(2,1)}, f32[1024,256]{1,0:T(8,128)S(1)}) fusion(bf16[256,256]{1,0:T(8,128)(2,1)S(1)} %copy-done, f32[1024,256]{1,0:T(8,128)} %all-reduce.2.cloned.1.call-done, f32[1024]{0:T(1024)S(1)} %add_rsqrt_fusion), kind=kOutput, calls=%fused_computation.5 | convolution fusion | flops 136052736 | bytes 2756608 | tf_op jit(solution)/shard_map/dot_general | solution.py:32
  109.2 0.0 copy-done.2
  109.2 0.0 copy-done.1
  109.2 1.5 fusion.3
  110.7 0.0 all-gather.6.cloned.1.call-update
  110.7 27.4 %all-gather.6.cloned.1.call-done = f32[2048,256]{1,0:T(8,128)} async-done(((f32[256,256]{1,0:T(8,128)}), f32[2048,256]{1,0:T(8,128)}) %all-gather.6.cloned.1.call-update) | async-done | bytes 2097168 | tf_op jit(solution)/shard_map/all_gather | solution.py:41
  138.2 2.5 %reduce_sum.19 = f32[256,256]{1,0:T(8,128)} reduce(f32[8,256,256]{2,1,0:T(8,128)} %bitcast.16, f32[]{:T(128)} %constant.56.clone.1), dimensions={0}, to_apply=%region_3.4 | reduce | flops 458752 | bytes 2359300 | tf_op jit(solution)/shard_map/reduce_sum | solution.py:42
  (3 shorter events, 0.0 us)
Async XLA Ops:
  7.2 99.5 %copy-start = (bf16[256,256]{1,0:T(8,128)(2,1)S(1)}, bf16[256,256]{1,0:T(8,128)(2,1)}, u32[]{:S(2)}) copy-start(bf16[256,256]{1,0:T(8,128)(2,1)} %param.7) | copy-start | bytes 393220
  7.2 42.2 %all-gather.4.cloned.1.call-start = ((), (), s32[]{:S(2)}) async-start(), calls=%async_computation | async-start | bytes 4718592 | tf_op jit(solution)/shard_map/all_gather | solution.py:16
  7.9 98.7 %all-reduce.2.cloned.1.call-start = ((), (), s32[]{:S(2)}) async-start(), calls=%async_computation.1 | async-start | bytes 2097152 | tf_op jit(solution)/shard_map/psum | solution.py:30
  54.5 83.6 %all-gather.6.cloned.1.call-start = ((), (), s32[]{:S(2)}) async-start(), calls=%async_computation.2 | async-start | bytes 2359296 | tf_op jit(solution)/shard_map/all_gather | solution.py:41
  68.5 40.8 %copy-start.2 = (bf16[1024,256]{1,0:T(8,128)(2,1)S(1)}, bf16[1024,256]{1,0:T(8,128)(2,1)}, u32[]{:S(2)}) copy-start(bf16[1024,256]{1,0:T(8,128)(2,1)} %param.8) | copy-start | bytes 1572868
  106.6 2.6 %copy-start.1 = (f32[1024,256]{1,0:T(8,128)S(1)}, f32[1024,256]{1,0:T(8,128)}, u32[]{:S(2)}) copy-start(f32[1024,256]{1,0:T(8,128)} %all-reduce.2.cloned.1.call-done) | copy-start | bytes 3145732
Sparse Core Ops, SparseCore 0:
  9.9 39.4 all-gather.3
  54.7 51.9 all-reduce.1
  110.8 27.2 all-gather.5
